TPU v7x, 32 devices: a whole 2x2x4 slice. The times are simulated.
32 devices in a mesh: grp: 2 (over y), ep: 8 (over z, x), tp: 2 (over core).
Axes of the slice: x: 2, y: 2, z: 4, core: 2. Of those that a mesh axis runs over, the one named last changes fastest.
Arguments:
- queries: bfloat16 [1024, 16, 576], P(('grp', 'ep'), 'tp'), parts along dimension 0, may hold values from -450 to 450
- latent_cache: bfloat16 [48, 512, 576], P(('grp', 'ep'), 'tp'), parts along dimension 0, may hold values from -6 to 6
- residual: bfloat16 [1024, 2048], P(('grp', 'ep')), parts along dimension 0, may hold values from -8 to 8
- token_request: int32 [1024], P(('grp', 'ep')), parts along dimension 0, may hold values from 0 to 2, as said below
- token_visible: int32 [1024], P(('grp', 'ep')), parts along dimension 0, may hold values from 1 to 512, as said below
- value_proj: bfloat16 [16, 512, 128], P('tp', 'ep'), may hold values from -0.25 to 0.25
- out_proj: bfloat16 [2048, 2048], P('tp', 'ep'), may hold values from -0.125 to 0.125
- norm_gain: float32 [2048], replicated, may hold values from 0.1 to 1.9
- router: bfloat16 [2048, 64], replicated, may hold values from -0.0390625 to 0.0390625
- expert_ids: int32 [1024, 6], P(('grp', 'ep')), parts along dimension 0, may hold values from 0 to 63, all different within a row; in each aligned block of 64 rows (0 to 63, 64 to 127, ...) at most 8 rows name the same one
- gate_weight: bfloat16 [128, 2048, 384], P('ep', None, 'tp'), may hold values from -0.125 to 0.125
- up_weight: bfloat16 [128, 2048, 384], P('ep', None, 'tp'), may hold values from -0.125 to 0.125
- down_weight: bfloat16 [128, 384, 2048], P('ep', 'tp'), may hold values from -0.21875 to 0.21875
Outputs:
- hidden: bfloat16 [1024, 2048], P(('grp', 'ep'), 'tp'), parts along dimension 0
- expert_out: bfloat16 [1024, 2048], P(('grp', 'ep'), 'tp'), parts along dimension 0
There are 2 independent parts, one for each index of `grp`. A program takes and returns all parts, laid end to end along the dimension named above; an argument that names none is the same for every part. Nothing has to cross between parts.
Inputs may be any that keep to these rules, and one draw needn't show every extreme that they name: `token_request`: in each ep block, 62 tokens belong to request 0, a prefill span, and each other request has exactly one token; the tokens' order in the block is arbitrary. `token_visible`: the span's tokens read consecutive counts s + 1 to s + 62; 512 is reached in every draw. `expert_ids`: each row names 6 different experts; among the 64 tokens of one ep index no expert is named by more than 8 tokens, and this bound is reached.
All inputs are finite; a program needn't handle non-finite values.
Results may differ from a plain program's by a relative error of at most 0.018.
Values may be sent and summed in bfloat16 or wider, within the bound.
A program may use at most 128 MiB of HBM per device.

v0:
```python
import jax
import jax.numpy as jnp
from jax import lax
from jax.sharding import PartitionSpec as P

LATENT = 512
VDIM = 128
EXPERTS = 64
TOPK = 6
GROUPS = 2
CAP = 8
PIECES = 128


score_scale = 192.0 ** (-0.5)
epsilon = 1e-06


def masked_scores(queries, block_rows, token_request, token_visible):
    per_request = block_rows.shape[1]
    flat_rows = block_rows.reshape(-1, block_rows.shape[2])
    scores = (
        jnp.einsum("thc,kc->thk", queries, flat_rows, preferred_element_type=jnp.float32)
        * score_scale
    )
    column = jnp.arange(flat_rows.shape[0], dtype=jnp.int32)
    owner_id = column // per_request
    position = column % per_request
    allowed = (owner_id[None, :] == token_request[:, None]) & (
        position[None, :] < token_visible[:, None]
    )
    return (jnp.where(allowed[:, None, :], scores, -jnp.inf), flat_rows)


def weighted_rows(scores, row_peak, flat_rows):
    weights = jnp.exp(scores - row_peak[:, :, None]).astype(jnp.bfloat16)
    totals = jnp.sum(weights.astype(jnp.float32), axis=2)
    summed = jnp.einsum(
        "thk,kc->thc", weights, flat_rows[:, :LATENT], preferred_element_type=jnp.float32
    )
    return (summed, totals)


def expert_block(arrived, gate_weight, up_weight, down_weight):
    gate_vals = jnp.einsum("prd,pdf->prf", arrived, gate_weight, preferred_element_type=jnp.float32)
    up_vals = jnp.einsum("prd,pdf->prf", arrived, up_weight, preferred_element_type=jnp.float32)
    activated = (jax.nn.silu(gate_vals) * up_vals).astype(jnp.bfloat16)
    return jnp.einsum(
        "prf,pfd->prd", activated, down_weight, preferred_element_type=jnp.float32
    ).astype(jnp.bfloat16)


def body(
    queries,
    latent_cache,
    residual,
    token_request,
    token_visible,
    value_proj,
    out_proj,
    norm_gain,
    router,
    expert_ids,
    gate_weight,
    up_weight,
    down_weight,
):
    all_rows = lax.all_gather(latent_cache, "tp", axis=1, tiled=True)
    scores, flat_rows = masked_scores(queries, all_rows, token_request, token_visible)
    summed, totals = weighted_rows(scores, jnp.max(scores, axis=2), flat_rows)
    context = (summed / totals[:, :, None]).astype(jnp.bfloat16)
    tokens_here = context.shape[0]
    heads_here = context.shape[1]
    head_values = jnp.einsum(
        "thl,hlv->thv",
        context,
        lax.all_gather(value_proj, "ep", axis=1, tiled=True),
        preferred_element_type=jnp.float32,
    )
    heads_out = head_values.astype(jnp.bfloat16).reshape(tokens_here, heads_here * VDIM)
    column_block = jnp.dot(
        lax.all_gather(heads_out, "ep", axis=0, tiled=True),
        out_proj,
        preferred_element_type=jnp.float32,
    )
    attention_part = lax.all_to_all(column_block, "ep", split_axis=0, concat_axis=1, tiled=True)
    attention = lax.psum(attention_part, "tp")
    hidden = (residual.astype(jnp.float32) + attention).astype(jnp.bfloat16)
    hidden_wide = hidden.astype(jnp.float32)
    normed = (
        hidden_wide
        * lax.rsqrt(jnp.mean(hidden_wide * hidden_wide, axis=1, keepdims=True) + epsilon)
        * norm_gain
    ).astype(jnp.bfloat16)
    logits = jnp.dot(normed, router, preferred_element_type=jnp.float32)
    gate_share = jax.nn.softmax(jnp.take_along_axis(logits, expert_ids, axis=1), axis=1).astype(
        jnp.bfloat16
    )
    flat_ids = expert_ids.reshape(-1)
    position_id = jnp.arange(flat_ids.shape[0], dtype=jnp.int32)
    earlier = (flat_ids[:, None] == flat_ids[None, :]) & (
        position_id[None, :] < position_id[:, None]
    )
    slot_ids = (flat_ids * CAP + jnp.sum(earlier.astype(jnp.int32), axis=1)).reshape(
        tokens_here, TOPK
    )
    targets = jnp.arange(EXPERTS * CAP, dtype=jnp.int32)
    matches = slot_ids[:, :, None] == targets[None, None, :]
    picker = jnp.any(matches, axis=1).T.astype(jnp.bfloat16)
    model_width = normed.shape[1]
    mixing = jnp.sum(
        jnp.where(matches, gate_share[:, :, None], jnp.zeros((), jnp.bfloat16)), axis=1
    )
    mixing = jnp.broadcast_to(
        mixing.reshape(tokens_here, EXPERTS, 1, CAP), (tokens_here, EXPERTS, GROUPS, CAP)
    ).reshape(tokens_here, PIECES * CAP)
    core_count = lax.axis_size("tp")
    half_width = model_width // core_count
    core_start = lax.axis_index("tp") * half_width
    outgoing = jnp.dot(picker, normed, preferred_element_type=jnp.float32).astype(jnp.bfloat16)
    outgoing = jnp.broadcast_to(
        outgoing.reshape(EXPERTS, 1, CAP, model_width), (EXPERTS, GROUPS, CAP, model_width)
    ).reshape(PIECES, CAP, model_width)
    arrived = lax.all_to_all(outgoing, "ep", split_axis=0, concat_axis=1, tiled=True)
    partial_out = expert_block(arrived, gate_weight, up_weight, down_weight)
    returned = lax.all_to_all(partial_out, "ep", split_axis=1, concat_axis=0, tiled=True)
    routed = jnp.dot(
        mixing, returned.reshape(PIECES * CAP, model_width), preferred_element_type=jnp.float32
    )
    expert_out = lax.psum_scatter(
        routed.astype(jnp.bfloat16), "tp", scatter_dimension=1, tiled=True
    )
    hidden_part = lax.dynamic_slice_in_dim(hidden, core_start, half_width, 1)
    return (hidden_part, expert_out)


def solution(mesh):
    return jax.shard_map(
        body,
        mesh=mesh,
        in_specs=(
            P(("grp", "ep"), "tp", None),
            P(("grp", "ep"), "tp", None),
            P(("grp", "ep"), None),
            P(("grp", "ep")),
            P(("grp", "ep")),
            P("tp", "ep", None),
            P("tp", "ep"),
            P(),
            P(),
            P(("grp", "ep"), None),
            P("ep", None, "tp"),
            P("ep", None, "tp"),
            P("ep", "tp", None),
        ),
        out_specs=(P(("grp", "ep"), "tp"), P(("grp", "ep"), "tp")),
        check_vma=False,
    )
```

profile of v0, /device:TPU:11, one launch (start us, length us, event | category | flops | bytes accessed | tf_op | source)
XLA Modules:
  0.0 395.0 jit_solution(957612986233958496)
XLA Ops:
  8.7 0.8 compare_and_fusion
  9.6 11.6 %all-gather.4.cloned.1.call-done = bf16[3,512,576]{1,2,0:T(8,128)(2,1)} async-done(((bf16[3,256,576]{1,2,0:T(8,128)(2,1)}), bf16[3,512,576]{1,2,0:T(8,128)(2,1)}) %all-gather.4.cloned.1.call-update) | async-done | bytes 1769488 | tf_op jit(solution)/shard_map/all_gather | solution.py:68
  21.1 2.7 copy.88
  23.9 3.2 convert_reduce_fusion
  27.1 34.1 %all-gather.6.cloned.1.call-done = bf16[8,512,128]{2,1,0:T(8,128)(2,1)} async-done(((bf16[8,64,128]{2,1,0:T(8,128)(2,1)}), bf16[8,512,128]{2,1,0:T(8,128)(2,1)}) %all-gather.6.cloned.1.call-update) | async-done | bytes 1048592 | tf_op jit(solution)/shard_map/all_gather | solution.py:77
  61.3 2.9 fusion.22
  65.0 39.1 %all-gather.8.cloned.1.call-done = bf16[512,1024]{1,0:T(8,128)(2,1)} async-done(((bf16[64,1024]{1,0:T(8,128)(2,1)}), bf16[512,1024]{1,0:T(8,128)(2,1)}) %all-gather.8.cloned.1.call-update) | async-done | bytes 1048592 | tf_op jit(solution)/shard_map/all_gather | solution.py:82
  104.1 1.7 fusion.54
  105.7 14.9 %all_to_all.52 = f32[8,64,256]{2,1,0:T(8,128)S(1)} all-to-all(f32[8,64,256]{2,1,0:T(8,128)S(1)} %bitcast.65), channel_id=1, replica_groups=mesh['grp'=2,'ep'=8,'tp'=2] {'ep'}, dimensions={0} | all-to-all | bytes 1048576 | tf_op jit(solution)/shard_map/all_to_all | solution.py:86
  120.6 0.9 copy.107
  122.4 21.3 %all-reduce.2.cloned.1.call-done = f32[64,2048]{1,0:T(8,128)} async-done(((f32[64,2048]{1,0:T(8,128)}), f32[64,2048]{1,0:T(8,128)}) %all-reduce.2.cloned.1.call-update) | async-done | bytes 524304 | tf_op jit(solution)/shard_map/psum | solution.py:87
  143.7 1.2 fusion.35
  144.9 0.8 fusion.11
  146.2 95.6 %all_to_all.53 = bf16[128,8,2048]{2,1,0:T(8,128)(2,1)S(1)} all-to-all(bf16[128,8,2048]{2,1,0:T(8,128)(2,1)S(1)} %bitcast.62), channel_id=1, replica_groups=mesh['grp'=2,'ep'=8,'tp'=2] {'ep'}, dimensions={0} | all-to-all | bytes 8388608 | tf_op jit(solution)/shard_map/all_to_all | solution.py:124
  241.8 2.0 copy-done.2
  243.8 10.0 %fusion.3 = f32[16,64,192]{2,1,0:T(8,128)} fusion(bf16[16,2048,192]{1,2,0:T(8,128)(2,1)} %param.23, bf16[16,8,8,2048]{3,2,0,1:T(8,128)(2,1)S(1)} %bitcast.59), kind=kOutput, calls=%fused_computation.4 | convolution fusion | flops 805306368 | bytes 17563648 | tf_op jit(solution)/shard_map/prd,pdf->prf/dot_general | solution.py:45
  253.8 14.3 %convolution_convert_fusion = bf16[16,64,2048]{2,1,0:T(8,128)(2,1)} fusion(bf16[16,192,2048]{2,1,0:T(8,128)(2,1)} %param.25, bf16[16,2048,192]{1,2,0:T(8,128)(2,1)} %param.24, bf16[16,8,8,2048]{3,2,0,1:T(8,128)(2,1)} %bitcast.60, f32[16,64,192]{2,1,0:T(8,128)} %fusion.3), kind=kOutput, calls=%fused_computation.7 | convolution fusion | flops 1613889536 | bytes 34340864 | tf_op jit(solution)/shard_map/prf,pfd->prd/dot_general | solution.py:48
  268.1 6.5 %copy.100 = bf16[16,64,2048]{2,0,1:T(8,128)(2,1)} copy(bf16[16,64,2048]{2,1,0:T(8,128)(2,1)} %convolution_convert_fusion) | data formatting | bytes 8388608 | tf_op jit(solution)/shard_map/convert_element_type | solution.py:50
  274.5 6.7 %all-to-all-start.2 = ((bf16[16,64,2048]{2,0,1:T(8,128)(2,1)}), bf16[16,64,2048]{2,0,1:T(8,128)(2,1)}, u32[]{:S(2)}, u32[]{:S(2)}) async-start(bf16[16,64,2048]{2,0,1:T(8,128)(2,1)} %copy.100), calls=%async_computation.2 | async-start | bytes 8388608 | tf_op jit(solution)/shard_map/all_to_all | solution.py:126
  281.8 2.9 gather_fusion
  285.2 86.6 %all-to-all-done.2 = bf16[16,64,2048]{2,0,1:T(8,128)(2,1)} async-done(((bf16[16,64,2048]{2,0,1:T(8,128)(2,1)}), bf16[16,64,2048]{2,0,1:T(8,128)(2,1)}, u32[]{:S(2)}, u32[]{:S(2)}) %all-to-all-start.2) | async-done | bytes 4194336 | tf_op jit(solution)/shard_map/all_to_all | solution.py:126
  371.8 4.7 %copy.102 = bf16[8,16,8,2048]{3,2,1,0:T(8,128)(2,1)S(1)} copy(bf16[8,16,8,2048]{3,1,2,0:T(8,128)(2,1)} %bitcast.16) | data formatting | bytes 8388608 | tf_op jit(solution)/shard_map/all_to_all | solution.py:126
  376.5 1.6 convolution_convert_fusion.2
  378.8 9.6 %reduce-scatter.2.cloned.1.call-done = bf16[64,1024]{1,0:T(8,128)(2,1)} async-done(((bf16[64,2048]{1,0:T(8,128)(2,1)}), bf16[64,1024]{1,0:T(8,128)(2,1)}) %reduce-scatter.2.cloned.1.call-update) | async-done | bytes 131088 | tf_op jit(solution)/shard_map/reduce_scatter | solution.py:130
  (50 shorter events, 5.6 us)
Async XLA Ops:
  7.2 16.7 %copy-start = (bf16[64,8,576]{2,1,0:T(8,128)(2,1)S(1)}, bf16[64,8,576]{2,1,0:T(8,128)(2,1)}, u32[]{:S(2)}) copy-start(bf16[64,8,576]{2,1,0:T(8,128)(2,1)} %param.13) | copy-start | bytes 1769476
  7.2 13.9 %all-gather.4.cloned.1.call-start = ((), (), s32[]{:S(2)}) async-start(), calls=%async_computation.4 | async-start | bytes 2654208 | tf_op jit(solution)/shard_map/all_gather | solution.py:68
  7.9 53.4 %all-gather.6.cloned.1.call-start = ((), (), s32[]{:S(2)}) async-start(), calls=%async_computation.5 | async-start | bytes 1179648 | tf_op jit(solution)/shard_map/all_gather | solution.py:77
  8.7 95.4 %all-gather.8.cloned.1.call-start = ((), (), s32[]{:S(2)}) async-start(), calls=%async_computation.6 | async-start | bytes 1179648 | tf_op jit(solution)/shard_map/all_gather | solution.py:82
  61.3 42.8 %copy-start.3 = (bf16[1024,256]{1,0:T(8,128)(2,1)S(1)}, bf16[1024,256]{1,0:T(8,128)(2,1)}, u32[]{:S(2)}) copy-start(bf16[1024,256]{1,0:T(8,128)(2,1)} %param.19) | copy-start | bytes 1572868
  64.2 57.3 %copy-start.5 = (s32[64,6]{0,1:T(8,128)S(1)}, s32[64,6]{0,1:T(8,128)}, u32[]{:S(2)}) copy-start(s32[64,6]{0,1:T(8,128)} %param.22) | copy-start | bytes 4612
  64.2 79.5 %copy-start.4 = (bf16[64,2048]{1,0:T(8,128)(2,1)S(1)}, bf16[64,2048]{1,0:T(8,128)(2,1)}, u32[]{:S(2)}) copy-start(bf16[64,2048]{1,0:T(8,128)(2,1)} %param.15) | copy-start | bytes 786436
  64.2 80.7 %copy-start.6 = (f32[2048]{0:T(1024)S(1)}, f32[2048]{0:T(1024)}, u32[]{:S(2)}) copy-start(f32[2048]{0:T(1024)} %param.20) | copy-start | bytes 24580
  64.9 78.7 %all-reduce.2.cloned.1.call-start = ((), (), s32[]{:S(2)}) async-start(), calls=%async_computation.7 | async-start | bytes 1048576 | tf_op jit(solution)/shard_map/psum | solution.py:87
  241.8 2.0 copy-start.2
  274.5 6.9 %copy-start.7 = (bf16[2048,64]{0,1:T(8,128)(2,1)S(1)}, bf16[2048,64]{0,1:T(8,128)(2,1)}, u32[]{:S(2)}) copy-start(bf16[2048,64]{0,1:T(8,128)(2,1)} %param.21) | copy-start | bytes 786436
  274.5 97.3 %all-to-all-start.2 = ((bf16[16,64,2048]{2,0,1:T(8,128)(2,1)}), bf16[16,64,2048]{2,0,1:T(8,128)(2,1)}, u32[]{:S(2)}, u32[]{:S(2)}) async-start(bf16[16,64,2048]{2,0,1:T(8,128)(2,1)} %copy.100), calls=%async_computation.2 | async-start | bytes 8388608 | tf_op jit(solution)/shard_map/all_to_all | solution.py:126
  281.2 107.2 %reduce-scatter.2.cloned.1.call-start = ((), (), s32[]{:S(2)}) async-start(), calls=%async_computation.8 | async-start | bytes 393216 | tf_op jit(solution)/shard_map/reduce_scatter | solution.py:130
  371.8 16.6 %copy-start.1 = (bf16[64,8,576]{2,1,0:T(8,128)(2,1)S(1)}, bf16[64,8,576]{2,1,0:T(8,128)(2,1)}, u32[]{:S(2)}) copy-start(bf16[64,8,576]{2,1,0:T(8,128)(2,1)} %param.13) | copy-start | bytes 1769476
Sparse Core Ops, SparseCore 0:
  9.5 11.5 all-gather.3
  23.3 37.9 all-gather.5
  65.0 38.9 all-gather.7
  121.6 21.9 all-reduce.1
  378.3 10.1 reduce-scatter.1
where the time goes:
time: 396 us; the launch traced here: 395 us
  waiting for transfers between devices  204 us (52%)
  blocking collectives  110 us (28%)
  matrix products  34.7 us (9%)
  local copies, waits for them, and re-layouts  22.6 us (6%)
  between operations  14 us (4%)
  starting transfers between devices  6.82 us (2%)
    all_to_all x1, blocking collectives, body(): lax.all_to_all(outgoing, 'ep', split_axis=0, concat_axis=1, tiled=True)  95.6 us
    all_to_all x1, waiting for transfers between devices, body(): lax.all_to_all(partial_out, 'ep', split_axis=1, concat_axis=0, tiled=True)  86.6 us
    all_gather x1, waiting for transfers between devices, body(): lax.all_gather(heads_out, 'ep', axis=0, tiled=True)  39.1 us
    all_gather x1, waiting for transfers between devices, body(): lax.all_gather(value_proj, 'ep', axis=1, tiled=True)  34.1 us
    psum x1, waiting for transfers between devices, body(): attention = lax.psum(attention_part, 'tp')  21.3 us
    all_to_all x1, blocking collectives, body(): lax.all_to_all(column_block, 'ep', split_axis=0, concat_axis=1, tiled=True)  14.9 us
    dot_general x1, matrix products, expert_block(): jnp.einsum('prf,pfd->prd', activated, down_weight, preferred_element_type...  14.3 us
    all_gather x1, waiting for transfers between devices, body(): all_rows = lax.all_gather(latent_cache, 'tp', axis=1, tiled=True)  11.6 us
  transfers between devices with their start and end apart: 6, of which 6 were waited for; matrix products, arithmetic and copies ran while one was open for 3% of the time, Pallas kernels for 0%

commit v1 on v0

--- a/solution.py
+++ b/solution.py
@@ -1,6 +1,10 @@
+import functools
+
 import jax
 import jax.numpy as jnp
 from jax import lax
+from jax.experimental import pallas as pl
+from jax.experimental.pallas import tpu as pltpu
 from jax.sharding import PartitionSpec as P
 
 LATENT = 512
@@ -10,6 +14,7 @@
 GROUPS = 2
 CAP = 8
 PIECES = 128
+MESH = pl.DeviceIdType.MESH
 
 
 score_scale = 192.0 ** (-0.5)
@@ -134,9 +139,437 @@
     return (hidden_part, expert_out)
 
 
+def ring_position(index, count):
+    half = lax.div(index, 2)
+    return half + lax.rem(index, 2) * (count - 1 - 2 * half)
+
+
+def ring_index(place, count):
+    place = lax.rem(place + count, count)
+    upper = lax.div(place, count // 2)
+    return 2 * place + upper * (2 * count - 1 - 4 * place)
+
+
+def greet(count):
+    me = lax.axis_index("ep")
+    core = lax.axis_index("tp")
+    barrier = pltpu.get_barrier_semaphore()
+    for step in range(1, count):
+        pl.semaphore_signal(
+            barrier, inc=1, device_id={"ep": lax.rem(me + step, count)}, device_id_type=MESH
+        )
+    pl.semaphore_signal(barrier, inc=1, device_id={"tp": 1 - core}, device_id_type=MESH)
+    pl.semaphore_wait(barrier, count)
+
+
+def remote(src, dst, send_sem, recv_sem, where):
+    return pltpu.make_async_remote_copy(
+        src_ref=src,
+        dst_ref=dst,
+        send_sem=send_sem,
+        recv_sem=recv_sem,
+        device_id=where,
+        device_id_type=MESH,
+    )
+
+
+def ring_gather(count, own, slot, send_sem, recv_sem, arrived):
+    me = lax.axis_index("ep")
+    place = ring_position(me, count)
+    reach = (count // 2, count - 1 - count // 2)
+    to = (ring_index(place + 1, count), ring_index(place - 1, count))
+
+    def hop(way, step):
+        sign = 1 if way == 0 else -1
+        block = ring_index(place - sign * (step - 1), count)
+        return remote(
+            own if step == 1 else slot(block),
+            slot(block),
+            send_sem.at[way, step - 1],
+            recv_sem.at[way, step - 1],
+            {"ep": to[way]},
+        )
+
+    hops = {}
+    for way in range(2):
+        if reach[way] >= 1:
+            hops[way, 1] = hop(way, 1)
+            hops[way, 1].start()
+    arrived(me, 0)
+    number = 1
+    for step in range(1, reach[0] + 1):
+        for way in range(2):
+            if step > reach[way]:
+                continue
+            hops[way, step].wait_recv()
+            if step < reach[way]:
+                hops[way, step + 1] = hop(way, step + 1)
+                hops[way, step + 1].start()
+            sign = 1 if way == 0 else -1
+            arrived(ring_index(place - sign * step, count), number)
+            number += 1
+    for copy in hops.values():
+        copy.wait_send()
+
+
+def gather_kernel(
+    count, cache_ref, value_ref, ids_ref, rows_ref, values_ref, all_ids_ref,
+    tp_send, tp_recv, ring_send, ring_recv, id_send, id_recv, own_sem,
+):
+    me = lax.axis_index("ep")
+    core = lax.axis_index("tp")
+    greet(count)
+    swap = remote(cache_ref, rows_ref.at[:, core], tp_send, tp_recv, {"tp": 1 - core})
+    swap.start()
+    owns = [
+        pltpu.make_async_copy(cache_ref, rows_ref.at[:, core], own_sem.at[0]),
+        pltpu.make_async_copy(value_ref, values_ref.at[:, me], own_sem.at[1]),
+        pltpu.make_async_copy(ids_ref, all_ids_ref.at[me], own_sem.at[2]),
+    ]
+    for copy in owns:
+        copy.start()
+    id_copies = [
+        remote(
+            ids_ref, all_ids_ref.at[me], id_send.at[step - 1], id_recv.at[step - 1],
+            {"ep": lax.rem(me + step, count)},
+        )
+        for step in range(1, count)
+    ]
+    for copy in id_copies:
+        copy.start()
+    ring_gather(
+        count, value_ref, lambda block: values_ref.at[:, block], ring_send, ring_recv,
+        lambda block, number: None,
+    )
+    for copy in id_copies:
+        copy.wait()
+    for copy in owns:
+        copy.wait()
+    swap.wait()
+
+
+def middle_kernel(
+    count, heads_ref, proj_ref, residual_ref, gain_ref, normed_ref, hidden_ref,
+    gathered, mine, theirs, outbox, inbox, hidden_own, normed_own,
+    ring_send, ring_recv, pair_send, pair_recv, back_send, back_recv,
+    ring2_send, ring2_recv, fwd_send, fwd_recv, own_sem, swap_send, swap_recv,
+):
+    me = lax.axis_index("ep")
+    core = lax.axis_index("tp")
+    tokens = heads_ref.shape[0]
+    half = tokens // 2
+    width = proj_ref.shape[1]
+    model = residual_ref.shape[1]
+    greet(count)
+    pairs = []
+
+    def project(block, number):
+        rows = heads_ref[...] if number == 0 else gathered[block]
+        product = jnp.dot(rows, proj_ref[...], preferred_element_type=jnp.float32)
+        mine[number] = product.reshape(2, half, width)
+        copy = remote(
+            mine.at[number, 1 - core], theirs.at[number], pair_send.at[number],
+            pair_recv.at[number], {"tp": 1 - core},
+        )
+        copy.start()
+        pairs.append((copy, block))
+
+    backs = []
+
+    def pass_back(number):
+        copy, block = pairs[number]
+        copy.wait_recv()
+        total = (mine[number, core] + theirs[number]).astype(jnp.bfloat16)
+        if number == 0:
+            inbox[me] = total
+        else:
+            outbox[number - 1] = total
+            back = remote(
+                outbox.at[number - 1], inbox.at[me], back_send.at[number - 1],
+                back_recv.at[number - 1], {"ep": block},
+            )
+            back.start()
+            backs.append(back)
+
+    def arrived(block, number):
+        project(block, number)
+        if number >= 1:
+            pass_back(number - 1)
+
+    ring_gather(count, heads_ref, lambda block: gathered.at[block], ring_send, ring_recv, arrived)
+    pass_back(count - 1)
+    for copy, _ in pairs:
+        copy.wait_send()
+    for back in backs:
+        back.wait()
+    attention = jnp.concatenate([inbox[i] for i in range(count)], axis=1).astype(jnp.float32)
+    hidden = (residual_ref[...].astype(jnp.float32) + attention).astype(jnp.bfloat16)
+    wide = hidden.astype(jnp.float32)
+    scale = lax.rsqrt(jnp.mean(wide * wide, axis=1, keepdims=True) + epsilon)
+    normed_own[...] = (wide * scale * gain_ref[...]).astype(jnp.bfloat16)
+    hidden_own[0] = hidden[:, : model // 2]
+    hidden_own[1] = hidden[:, model // 2 :]
+    swap = remote(
+        hidden_own.at[1 - core], hidden_ref.at[core], swap_send, swap_recv, {"tp": 1 - core}
+    )
+    swap.start()
+    owns = [
+        pltpu.make_async_copy(hidden_own.at[core], hidden_ref.at[core], own_sem.at[0]),
+        pltpu.make_async_copy(normed_own, normed_ref.at[me, core], own_sem.at[1]),
+    ]
+    for copy in owns:
+        copy.start()
+    forwards = []
+
+    def forward(block, number):
+        source = normed_own if number == 0 else normed_ref.at[block, core]
+        copy = remote(
+            source, normed_ref.at[block, core], fwd_send.at[number], fwd_recv.at[number],
+            {"tp": 1 - core},
+        )
+        copy.start()
+        forwards.append(copy)
+
+    ring_gather(
+        count, normed_own, lambda block: normed_ref.at[block, core], ring2_send, ring2_recv, forward
+    )
+    for copy in forwards:
+        copy.wait()
+    for copy in owns:
+        copy.wait()
+    swap.wait()
+
+
+def return_kernel(
+    count, sums_ref, out_ref, theirs, outbox, inbox, pair_send, pair_recv, back_send, back_recv
+):
+    me = lax.axis_index("ep")
+    core = lax.axis_index("tp")
+    greet(count)
+    order = [lax.rem(me + step, count) for step in list(range(1, count)) + [0]]
+    pairs = []
+    for number, block in enumerate(order):
+        copy = remote(
+            sums_ref.at[1 - core, block], theirs.at[number], pair_send.at[number],
+            pair_recv.at[number], {"tp": 1 - core},
+        )
+        copy.start()
+        pairs.append(copy)
+    backs = []
+    for number, block in enumerate(order):
+        pairs[number].wait_recv()
+        total = sums_ref[core, block].astype(jnp.float32) + theirs[number].astype(jnp.float32)
+        if number < count - 1:
+            outbox[number] = total.astype(jnp.bfloat16)
+            back = remote(
+                outbox.at[number], inbox.at[number], back_send.at[number], back_recv.at[number],
+                {"ep": block},
+            )
+            back.start()
+            backs.append(back)
+    for number, back in enumerate(backs):
+        back.wait_recv()
+        total = total + inbox[number].astype(jnp.float32)
+    out_ref[...] = total.astype(jnp.bfloat16)
+    for copy in pairs:
+        copy.wait_send()
+    for back in backs:
+        back.wait_send()
+
+
+def expert_kernel(blocks, rows_ref, gate_ref, up_ref, down_ref, out_ref):
+    rows = rows_ref[0]
+    total = None
+    for block in range(blocks):
+        gate = jnp.dot(rows, gate_ref[block], preferred_element_type=jnp.float32)
+        up = jnp.dot(rows, up_ref[block], preferred_element_type=jnp.float32)
+        activated = (gate / (1.0 + jnp.exp(-gate)) * up).astype(jnp.bfloat16)
+        part = jnp.dot(activated, down_ref[block], preferred_element_type=jnp.float32)
+        total = part if total is None else total + part
+    out_ref[0] = total.astype(jnp.bfloat16)
+
+
+def vmem_call(kernel, outs, scratch, ident, *args):
+    whole = pl.BlockSpec(memory_space=pltpu.VMEM)
+    return pl.pallas_call(
+        kernel,
+        out_shape=outs,
+        in_specs=[whole] * len(args),
+        out_specs=jax.tree.map(lambda _: whole, outs),
+        scratch_shapes=scratch,
+        compiler_params=pltpu.CompilerParams(
+            collective_id=ident, has_side_effects=True, vmem_limit_bytes=40 * 2**20
+        ),
+    )(*args)
+
+
+def dma(*shape):
+    return pltpu.SemaphoreType.DMA(shape)
+
+
+def lean_body(
+    queries,
+    latent_cache,
+    residual,
+    token_request,
+    token_visible,
+    value_proj,
+    out_proj,
+    norm_gain,
+    router,
+    expert_ids,
+    gate_weight,
+    up_weight,
+    down_weight,
+):
+    count = lax.axis_size("ep")
+    core = lax.axis_index("tp")
+    me = lax.axis_index("ep")
+    tokens, heads = queries.shape[:2]
+    half = tokens // 2
+    requests, positions, columns = latent_cache.shape
+    model = residual.shape[1]
+    bf16 = jnp.bfloat16
+    shape = jax.ShapeDtypeStruct
+    reach = max(1, count // 2)
+
+    id_rows = -(-tokens * TOPK // 1024) * 8
+    flat_ids = jnp.pad(expert_ids.reshape(-1), (0, id_rows * 128 - tokens * TOPK))
+    rows, values, all_ids = vmem_call(
+        functools.partial(gather_kernel, count),
+        (
+            shape((requests, 2, positions, columns), bf16),
+            shape((value_proj.shape[0], count) + value_proj.shape[1:], bf16),
+            shape((count, id_rows, 128), jnp.int32),
+        ),
+        [
+            dma(), dma(), dma(2, reach), dma(2, reach), dma(count - 1), dma(count - 1), dma(3),
+        ],
+        0,
+        latent_cache, value_proj, flat_ids.reshape(id_rows, 128),
+    )
+    scores, flat_rows = masked_scores(
+        queries, rows.reshape(requests, 2 * positions, columns), token_request, token_visible
+    )
+    summed, totals = weighted_rows(scores, jnp.max(scores, axis=2), flat_rows)
+    context = (summed / totals[:, :, None]).astype(bf16)
+    head_values = jnp.einsum(
+        "thl,hlv->thv",
+        context,
+        values.reshape(heads, LATENT, VDIM),
+        preferred_element_type=jnp.float32,
+    )
+    heads_out = head_values.astype(bf16).reshape(tokens, heads * VDIM)
+    width = out_proj.shape[1]
+    normed, hidden = vmem_call(
+        functools.partial(middle_kernel, count),
+        (shape((count, 2, half, model), bf16), shape((2, half, model // 2), bf16)),
+        [
+            pltpu.VMEM((count, tokens, heads * VDIM), bf16),
+            pltpu.VMEM((count, 2, half, width), jnp.float32),
+            pltpu.VMEM((count, half, width), jnp.float32),
+            pltpu.VMEM((count - 1, half, width), bf16),
+            pltpu.VMEM((count, half, width), bf16),
+            pltpu.VMEM((2, half, model // 2), bf16),
+            pltpu.VMEM((half, model), bf16),
+            dma(2, reach), dma(2, reach), dma(count), dma(count), dma(count - 1), dma(count - 1),
+            dma(2, reach), dma(2, reach), dma(count), dma(count), dma(2), dma(), dma(),
+        ],
+        1,
+        heads_out,
+        out_proj,
+        lax.dynamic_slice_in_dim(residual, core * half, half, 0),
+        norm_gain.reshape(1, model),
+    )
+    normed = normed.reshape(count * tokens, model)
+
+    local = EXPERTS // count
+    ids = all_ids.reshape(count, -1)[:, : tokens * TOPK].reshape(count * tokens, TOPK)
+    named = jnp.any(ids[:, :, None] == jnp.arange(EXPERTS, dtype=jnp.int32), axis=1)
+    logits = jnp.dot(normed, router, preferred_element_type=jnp.float32)
+    logits = jnp.where(named, logits, -jnp.inf)
+    raised = jnp.exp(logits - jnp.max(logits, axis=1, keepdims=True))
+    share = (raised / jnp.sum(raised, axis=1, keepdims=True)).astype(bf16)
+    first = me * local
+    here = lax.dynamic_slice_in_dim(named, first, local, 1)
+    share_here = lax.dynamic_slice_in_dim(share, first, local, 1)
+    before = jnp.tril(jnp.ones((tokens, tokens), bf16), -1)
+    ranks = jnp.einsum(
+        "st,bte->bse",
+        before,
+        here.reshape(count, tokens, local).astype(bf16),
+        preferred_element_type=jnp.float32,
+    ).astype(jnp.int32)
+    source = jnp.arange(count, dtype=jnp.int32)
+    place = (ranks + source[:, None, None] * CAP).reshape(count * tokens, local)
+    hits = here[:, :, None] & (place[:, :, None] == jnp.arange(count * CAP, dtype=jnp.int32))
+    mixing = jnp.where(hits, share_here[:, :, None], jnp.zeros((), bf16))
+    picked = jnp.einsum(
+        "tes,td->esd", hits.astype(bf16), normed, preferred_element_type=jnp.float32
+    ).astype(bf16)
+
+    slots = count * CAP
+    blocks = gate_weight.shape[0] // local
+    hidden_here = gate_weight.shape[2]
+    expert_rows = pl.pallas_call(
+        functools.partial(expert_kernel, blocks),
+        grid=(local,),
+        out_shape=shape((local, slots, model), bf16),
+        in_specs=[
+            pl.BlockSpec((1, slots, model), lambda e: (e, 0, 0)),
+            pl.BlockSpec((blocks, model, hidden_here), lambda e: (e, 0, 0)),
+            pl.BlockSpec((blocks, model, hidden_here), lambda e: (e, 0, 0)),
+            pl.BlockSpec((blocks, hidden_here, model), lambda e: (e, 0, 0)),
+        ],
+        out_specs=pl.BlockSpec((1, slots, model), lambda e: (e, 0, 0)),
+        compiler_params=pltpu.CompilerParams(vmem_limit_bytes=40 * 2**20),
+    )(picked, gate_weight, up_weight, down_weight)
+    sums = [
+        jnp.einsum(
+            "tes,esd->td",
+            mixing,
+            expert_rows[:, :, side * (model // 2) : (side + 1) * (model // 2)],
+            preferred_element_type=jnp.float32,
+        ).astype(bf16)
+        for side in range(2)
+    ]
+    sums = jnp.stack(sums).reshape(2, count, tokens, model // 2)
+    block = (tokens, model // 2)
+    expert_out = vmem_call(
+        functools.partial(return_kernel, count),
+        shape(block, bf16),
+        [
+            pltpu.VMEM((count,) + block, bf16),
+            pltpu.VMEM((count - 1,) + block, bf16),
+            pltpu.VMEM((count - 1,) + block, bf16),
+            dma(count), dma(count), dma(count - 1), dma(count - 1),
+        ],
+        2,
+        sums,
+    )
+    return (hidden.reshape(tokens, model // 2), expert_out)
+
+
+LEAN_BYTES = 8 * 2**20
+
+
+def choose(mesh):
+    count = mesh.shape["ep"]
+
+    def layer(*args):
+        tokens, model = args[2].shape
+        fits = count * tokens * model * 2 <= LEAN_BYTES
+        even = count % 2 == 0 and tokens % 32 == 0 and EXPERTS % count == 0
+        if fits and even and mesh.shape["tp"] == 2:
+            return lean_body(*args)
+        return body(*args)
+
+    return layer
+
+
 def solution(mesh):
     return jax.shard_map(
-        body,
+        choose(mesh),
         mesh=mesh,
         in_specs=(
             P(("grp", "ep"), "tp", None),

time: 396 us -> 178 us (0.45)
  waiting for transfers between devices: 204 us -> 0 us
  Pallas kernels: 0 us -> 114 us
  blocking collectives: 110 us -> 0 us
  local copies, waits for them, and re-layouts: 22.6 us -> 48.8 us
  matrix products: 34.7 us -> 11.4 us
  between operations: 14 us -> 0.88 us
  starting transfers between devices: 6.82 us -> 0 us
    pallas_call x0 -> x4, Pallas kernels: none -> 114 us  [the longest x3 96.7 us: vmem_call(): pl.pallas_call(kernel, out_shape=outs, in_specs=[whole] * len(args), out_...]
    all_to_all x2 -> x0, blocking collectives: 110 us -> none  [the longest x1 95.6 us: body(): lax.all_to_all(outgoing, 'ep', split_axis=0, concat_axis=1, tiled=True)]
    all_to_all x1 -> x0, waiting for transfers between devices: 86.6 us -> none  [body(): lax.all_to_all(partial_out, 'ep', split_axis=1, concat_axis=0, tiled=True)]
    all_gather x3 -> x0, waiting for transfers between devices: 84.8 us -> none  [the longest x1 39.1 us: body(): lax.all_gather(heads_out, 'ep', axis=0, tiled=True)]
    unnamed x17 -> x25, local copies, waits for them, and re-layouts: 2.11 us -> 47.2 us
    dot_general x7 -> x6, matrix products: 31.5 us -> 6.62 us  [the longest x1 2.89 us: lean_body(): jnp.einsum('thl,hlv->thv', context, values.reshape(heads, LATENT, VDIM),...]
    psum x1 -> x0, waiting for transfers between devices: 21.3 us -> none  [body(): attention = lax.psum(attention_part, 'tp')]
    reduce_scatter x1 -> x0, waiting for transfers between devices: 9.63 us -> none  [body(): lax.psum_scatter(routed.astype(jnp.bfloat16), 'tp', scatter_dimension=1,...]
  transfers between devices with their start and end apart: 6 -> 0, of which waited for: 6 -> 0; matrix products, arithmetic and copies ran while one was open for 3% -> 0% of each run, Pallas kernels for 0% -> 0%
where the time goes in v1:
time: 178 us; the launch traced here: 177 us
  Pallas kernels  114 us (64%)
  local copies, waits for them, and re-layouts  48.8 us (27%)
  matrix products  11.4 us (6%)
    pallas_call x3, Pallas kernels, vmem_call(): pl.pallas_call(kernel, out_shape=outs, in_specs=[whole] * len(args), out_...  96.7 us
    unnamed x25, local copies, waits for them, and re-layouts  47.2 us
    pallas_call x1, Pallas kernels, lean_body(): pl.pallas_call(functools.partial(expert_kernel, blocks), grid=(local,), o...  17.8 us
    sub x1, matrix products, weighted_rows(): weights = jnp.exp(scores - row_peak[:, :, None]).astype(jnp.bfloat16)  4.82 us

profile of v1, /device:TPU:11, one launch (start us, length us, event | category | flops | bytes accessed | tf_op | source)
XLA Modules:
  0.0 176.8 jit_solution(3364553377542145059)
XLA Ops:
  0.7 0.9 copy.30
  1.6 0.1 reshape.118
  1.7 0.8 compare_and_fusion
  2.5 0.9 constant_dynamic-slice_fusion.1.residual_ref
  3.5 1.5 copy.31.cache_ref
  5.0 16.6 %shard_map.140 = (bf16[3,2,256,576]{3,2,1,0:T(8,128)(2,1)S(1)}, bf16[8,8,64,128]{3,2,1,0:T(8,128)(2,1)S(1)}, s32[8,8,128]{2,1,0:T(8,128)S(1)}) custom-call(bf16[3,256,576]{2,1,0:T(8,128)(2,1)S(1)} %copy.31.cache_ref, bf16[8,64,128]{2,1,0:T(8,128)(2,1)S(1)} %copy-done.3, s32[8,128]{1,0:T(8,128)S(1)} %pad_bitcast_fusion.ids_ref), custom_call_target="tpu_custom_call" | custom-call | tf_op jit(solution)/shard_map/pallas_call | solution.py:394
  21.6 1.3 copy-done.5
  22.9 1.0 copy-done.7
  23.8 0.2 eq.52
  24.4 0.2 fusion.6
  24.7 4.8 %convert_reduce_fusion = (f32[64,8]{0,1:T(8,128)S(1)}, bf16[64,8,1536]{2,0,1:T(8,128)(2,1)}) fusion(bf16[1536,576,1]{1,0,2:T(8,128)(2,1)} %bitcast.63, pred[64,1536]{1,0:T(8,128)(4,1)S(1)} %compare_and_fusion, bf16[64,8,576]{2,1,0:T(8,128)(2,1)S(1)} %copy-done), kind=kOutput, calls=%fused_computation.3 | convolution fusion | flops 910689792 | bytes 4032512 | tf_op jit(solution)/shard_map/sub | solution.py:41
  29.5 2.9 %fusion.4 = bf16[8,8,8,128]{3,2,1,0:T(8,128)(2,1)S(1)} fusion(bf16[8,512,128]{2,1,0:T(8,128)(2,1)} %bitcast.65, bf16[64,8,1536]{2,0,1:T(8,128)(2,1)} %get-tuple-element.15, bf16[1536,576]{1,0:T(8,128)(2,1)S(1)} %bitcast.64, f32[64,8]{0,1:T(8,128)S(1)} %get-tuple-element.14), kind=kOutput, calls=%fused_computation.14 | convolution fusion | flops 873005056 | bytes 4329472 | tf_op jit(solution)/shard_map/thl,hlv->thv/dot_general | solution.py:456
  32.5 49.0 %shard_map.141 = (bf16[8,2,32,2048]{3,2,1,0:T(8,128)(2,1)S(1)}, bf16[2,32,1024]{2,1,0:T(8,128)(2,1)S(1)}) custom-call(bf16[64,1024]{1,0:T(8,128)(2,1)S(1)} %bitcast.59, bf16[1024,256]{1,0:T(8,128)(2,1)S(1)} %copy-done.2, bf16[32,2048]{1,0:T(8,128)(2,1)S(1)} %constant_dynamic-slice_fusion.1.residual_ref, f32[1,2048]{1,0:T(1,128)S(1)} %bitcast.62), custom_call_target="tpu_custom_call" | custom-call | tf_op jit(solution)/shard_map/pallas_call | solution.py:394
  81.5 0.8 fusion.49
  82.4 1.3 convolution_convert_fusion.rows_ref
  83.6 20.6 %copy.38.gate_ref = bf16[16,2048,192]{2,1,0:T(8,128)(2,1)} copy(bf16[16,2048,192]{1,2,0:T(8,128)(2,1)} %param.23) | data formatting | bytes 25165824 | tf_op args[10]
  104.2 20.6 %copy.39.up_ref = bf16[16,2048,192]{2,1,0:T(8,128)(2,1)} copy(bf16[16,2048,192]{1,2,0:T(8,128)(2,1)} %param.24) | data formatting | bytes 25165824 | tf_op args[11]
  124.8 17.8 %shard_map.142 = bf16[8,64,2048]{2,1,0:T(8,128)(2,1)S(1)} custom-call(bf16[8,64,2048]{2,1,0:T(8,128)(2,1)S(1)} %convolution_convert_fusion.rows_ref, bf16[16,2048,192]{2,1,0:T(8,128)(2,1)} %copy.38.gate_ref, bf16[16,2048,192]{2,1,0:T(8,128)(2,1)} %copy.39.up_ref, bf16[16,192,2048]{2,1,0:T(8,128)(2,1)} %down_ref.1), custom_call_target="tpu_custom_call" | custom-call | tf_op jit(solution)/shard_map/pallas_call | solution.py:514
  142.7 0.7 bitcast_convert_fusion
  143.4 0.7 bitcast_convert_fusion.1
  144.2 0.2 pad_maximum_fusion.sums_ref
  144.4 31.1 %shard_map.143 = bf16[64,1024]{1,0:T(8,128)(2,1)S(1)} custom-call(bf16[2,8,64,1024]{3,2,1,0:T(8,128)(2,1)S(1)} %pad_maximum_fusion.sums_ref), custom_call_target="tpu_custom_call" | custom-call | tf_op jit(solution)/shard_map/pallas_call | solution.py:394
  175.5 0.7 copy.56
  176.2 0.7 copy.57
  (31 shorter events, 0.6 us)
Async XLA Ops:
  0.6 24.1 %copy-start = (bf16[64,8,576]{2,1,0:T(8,128)(2,1)S(1)}, bf16[64,8,576]{2,1,0:T(8,128)(2,1)}, u32[]{:S(2)}) copy-start(bf16[64,8,576]{2,1,0:T(8,128)(2,1)} %param.13) | copy-start | bytes 1769476
  0.6 4.4 %copy-start.3 = (bf16[8,64,128]{2,1,0:T(8,128)(2,1)S(1)}, bf16[8,64,128]{2,1,0:T(8,128)(2,1)}, u32[]{:S(2)}) copy-start(bf16[8,64,128]{2,1,0:T(8,128)(2,1)} %value_ref.1) | copy-start | bytes 393220
  21.6 1.3 copy-start.5
  22.9 1.0 copy-start.7
  24.7 4.8 %copy-start.6 = (bf16[3,2,256,576]{3,2,1,0:T(8,128)(2,1)S(1)}, bf16[3,2,256,576]{3,2,1,0:T(8,128)(2,1)}, u32[]{:S(2)}) copy-start(bf16[3,2,256,576]{3,2,1,0:T(8,128)(2,1)} %copy-done.5) | copy-start | bytes 5308420
  29.5 2.9 %copy-start.2 = (bf16[1024,256]{1,0:T(8,128)(2,1)S(1)}, bf16[1024,256]{1,0:T(8,128)(2,1)}, u32[]{:S(2)}) copy-start(bf16[1024,256]{1,0:T(8,128)(2,1)} %proj_ref.1) | copy-start | bytes 1572868
  29.5 2.9 %copy-start.4 = (f32[2048]{0:T(1024)S(1)}, f32[2048]{0:T(1024)}, u32[]{:S(2)}) copy-start(f32[2048]{0:T(1024)} %param.20) | copy-start | bytes 24580
  29.5 52.0 %copy-start.8 = (bf16[2048,64]{0,1:T(8,128)(2,1)S(1)}, bf16[2048,64]{0,1:T(8,128)(2,1)}, u32[]{:S(2)}) copy-start(bf16[2048,64]{0,1:T(8,128)(2,1)} %param.21) | copy-start | bytes 786436
  144.2 32.6 %copy-start.1 = (bf16[64,8,576]{2,1,0:T(8,128)(2,1)S(1)}, bf16[64,8,576]{2,1,0:T(8,128)(2,1)}, u32[]{:S(2)}) copy-start(bf16[64,8,576]{2,1,0:T(8,128)(2,1)} %param.13) | copy-start | bytes 1769476

commit v2 on v1

--- a/solution.py
+++ b/solution.py
@@ -176,37 +176,45 @@
 def ring_gather(count, own, slot, send_sem, recv_sem, arrived):
     me = lax.axis_index("ep")
     place = ring_position(me, count)
-    reach = (count // 2, count - 1 - count // 2)
+    far = count // 2
+    near = count - 1 - far
     to = (ring_index(place + 1, count), ring_index(place - 1, count))
 
-    def hop(way, step):
-        sign = 1 if way == 0 else -1
-        block = ring_index(place - sign * (step - 1), count)
-        return remote(
-            own if step == 1 else slot(block),
-            slot(block),
-            send_sem.at[way, step - 1],
-            recv_sem.at[way, step - 1],
+    def reach(way, part):
+        return far if way == part else near
+
+    def origin(way, step):
+        return ring_index(place - step if way == 0 else place + step, count)
+
+    hops = {}
+
+    def hop(way, step, part):
+        if step > reach(way, part):
+            return
+        block = origin(way, step - 1)
+        hops[way, step, part] = remote(
+            own(part) if step == 1 else slot(block, part),
+            slot(block, part),
+            send_sem.at[way, step - 1, part],
+            recv_sem.at[way, step - 1, part],
             {"ep": to[way]},
         )
-
-    hops = {}
-    for way in range(2):
-        if reach[way] >= 1:
-            hops[way, 1] = hop(way, 1)
-            hops[way, 1].start()
+        hops[way, step, part].start()
+
+    for turn in range(2):
+        for way in range(2):
+            hop(way, 1, (way + turn) % 2)
     arrived(me, 0)
     number = 1
-    for step in range(1, reach[0] + 1):
-        for way in range(2):
-            if step > reach[way]:
-                continue
-            hops[way, step].wait_recv()
-            if step < reach[way]:
-                hops[way, step + 1] = hop(way, step + 1)
-                hops[way, step + 1].start()
-            sign = 1 if way == 0 else -1
-            arrived(ring_index(place - sign * step, count), number)
+    for step in range(1, far + 1):
+        for turn in range(2):
+            for way in range(2):
+                part = (way + turn) % 2
+                if step <= reach(way, part):
+                    hops[way, step, part].wait_recv()
+                    hop(way, step + 1, part)
+        for way in range(2 if step <= near else 1):
+            arrived(origin(way, step), number)
             number += 1
     for copy in hops.values():
         copy.wait_send()
@@ -218,6 +226,7 @@
 ):
     me = lax.axis_index("ep")
     core = lax.axis_index("tp")
+    some = value_ref.shape[0] // 2
     greet(count)
     swap = remote(cache_ref, rows_ref.at[:, core], tp_send, tp_recv, {"tp": 1 - core})
     swap.start()
@@ -238,7 +247,11 @@
     for copy in id_copies:
         copy.start()
     ring_gather(
-        count, value_ref, lambda block: values_ref.at[:, block], ring_send, ring_recv,
+        count,
+        lambda part: value_ref.at[pl.ds(part * some, some)],
+        lambda block, part: values_ref.at[pl.ds(part * some, some), block],
+        ring_send,
+        ring_recv,
         lambda block, number: None,
     )
     for copy in id_copies:
@@ -296,7 +309,14 @@
         if number >= 1:
             pass_back(number - 1)
 
-    ring_gather(count, heads_ref, lambda block: gathered.at[block], ring_send, ring_recv, arrived)
+    ring_gather(
+        count,
+        lambda part: heads_ref.at[pl.ds(part * half, half)],
+        lambda block, part: gathered.at[block, pl.ds(part * half, half)],
+        ring_send,
+        ring_recv,
+        arrived,
+    )
     pass_back(count - 1)
     for copy, _ in pairs:
         copy.wait_send()
@@ -330,8 +350,14 @@
         copy.start()
         forwards.append(copy)
 
+    some = half // 2
     ring_gather(
-        count, normed_own, lambda block: normed_ref.at[block, core], ring2_send, ring2_recv, forward
+        count,
+        lambda part: normed_own.at[pl.ds(part * some, some)],
+        lambda block, part: normed_ref.at[block, core, pl.ds(part * some, some)],
+        ring2_send,
+        ring2_recv,
+        forward,
     )
     for copy in forwards:
         copy.wait()
@@ -341,12 +367,16 @@
 
 
 def return_kernel(
-    count, sums_ref, out_ref, theirs, outbox, inbox, pair_send, pair_recv, back_send, back_recv
+    count, sums_ref, out_ref, theirs, outbox, inbox, outbox2, inbox2,
+    pair_send, pair_recv, cross_send, cross_recv, back_send, back_recv,
 ):
     me = lax.axis_index("ep")
     core = lax.axis_index("tp")
+    half = count // 2
+    twin = me + 1 - 2 * lax.rem(me, 2)
     greet(count)
-    order = [lax.rem(me + step, count) for step in list(range(1, count)) + [0]]
+    steps = list(range(1, half)) + [0]
+    order = [lax.rem(start + 2 * step, count) for start in (twin, me) for step in steps]
     pairs = []
     for number, block in enumerate(order):
         copy = remote(
@@ -355,34 +385,53 @@
         )
         copy.start()
         pairs.append(copy)
+
+    def both(number):
+        pairs[number].wait_recv()
+        return sums_ref[core, order[number]].astype(jnp.float32) + theirs[number].astype(
+            jnp.float32
+        )
+
+    crosses = []
+    for number in range(half):
+        outbox[number] = both(number).astype(jnp.bfloat16)
+        cross = remote(
+            outbox.at[number], inbox.at[number], cross_send.at[number], cross_recv.at[number],
+            {"ep": twin},
+        )
+        cross.start()
+        crosses.append(cross)
     backs = []
-    for number, block in enumerate(order):
-        pairs[number].wait_recv()
-        total = sums_ref[core, block].astype(jnp.float32) + theirs[number].astype(jnp.float32)
-        if number < count - 1:
-            outbox[number] = total.astype(jnp.bfloat16)
+    for number in range(half):
+        total = both(half + number)
+        crosses[number].wait_recv()
+        total = total + inbox[number].astype(jnp.float32)
+        if number < half - 1:
+            outbox2[number] = total.astype(jnp.bfloat16)
             back = remote(
-                outbox.at[number], inbox.at[number], back_send.at[number], back_recv.at[number],
-                {"ep": block},
+                outbox2.at[number], inbox2.at[number], back_send.at[number],
+                back_recv.at[number], {"ep": order[half + number]},
             )
             back.start()
             backs.append(back)
     for number, back in enumerate(backs):
         back.wait_recv()
-        total = total + inbox[number].astype(jnp.float32)
+        total = total + inbox2[number].astype(jnp.float32)
     out_ref[...] = total.astype(jnp.bfloat16)
-    for copy in pairs:
+    for copy in pairs + crosses + backs:
         copy.wait_send()
-    for back in backs:
-        back.wait_send()
 
 
 def expert_kernel(blocks, rows_ref, gate_ref, up_ref, down_ref, out_ref):
     rows = rows_ref[0]
     total = None
     for block in range(blocks):
-        gate = jnp.dot(rows, gate_ref[block], preferred_element_type=jnp.float32)
-        up = jnp.dot(rows, up_ref[block], preferred_element_type=jnp.float32)
+        gate = lax.dot_general(
+            rows, gate_ref[block], (((1,), (1,)), ((), ())), preferred_element_type=jnp.float32
+        )
+        up = lax.dot_general(
+            rows, up_ref[block], (((1,), (1,)), ((), ())), preferred_element_type=jnp.float32
+        )
         activated = (gate / (1.0 + jnp.exp(-gate)) * up).astype(jnp.bfloat16)
         part = jnp.dot(activated, down_ref[block], preferred_element_type=jnp.float32)
         total = part if total is None else total + part
@@ -443,7 +492,7 @@
             shape((count, id_rows, 128), jnp.int32),
         ),
         [
-            dma(), dma(), dma(2, reach), dma(2, reach), dma(count - 1), dma(count - 1), dma(3),
+            dma(), dma(), dma(2, reach, 2), dma(2, reach, 2), dma(count - 1), dma(count - 1), dma(3),
         ],
         0,
         latent_cache, value_proj, flat_ids.reshape(id_rows, 128),
@@ -472,8 +521,8 @@
             pltpu.VMEM((count, half, width), bf16),
             pltpu.VMEM((2, half, model // 2), bf16),
             pltpu.VMEM((half, model), bf16),
-            dma(2, reach), dma(2, reach), dma(count), dma(count), dma(count - 1), dma(count - 1),
-            dma(2, reach), dma(2, reach), dma(count), dma(count), dma(2), dma(), dma(),
+            dma(2, reach, 2), dma(2, reach, 2), dma(count), dma(count), dma(count - 1), dma(count - 1),
+            dma(2, reach, 2), dma(2, reach, 2), dma(count), dma(count), dma(2), dma(), dma(),
         ],
         1,
         heads_out,
@@ -517,13 +566,13 @@
         out_shape=shape((local, slots, model), bf16),
         in_specs=[
             pl.BlockSpec((1, slots, model), lambda e: (e, 0, 0)),
-            pl.BlockSpec((blocks, model, hidden_here), lambda e: (e, 0, 0)),
-            pl.BlockSpec((blocks, model, hidden_here), lambda e: (e, 0, 0)),
+            pl.BlockSpec((blocks, hidden_here, model), lambda e: (e, 0, 0)),
+            pl.BlockSpec((blocks, hidden_here, model), lambda e: (e, 0, 0)),
             pl.BlockSpec((blocks, hidden_here, model), lambda e: (e, 0, 0)),
         ],
         out_specs=pl.BlockSpec((1, slots, model), lambda e: (e, 0, 0)),
         compiler_params=pltpu.CompilerParams(vmem_limit_bytes=40 * 2**20),
-    )(picked, gate_weight, up_weight, down_weight)
+    )(picked, jnp.swapaxes(gate_weight, 1, 2), jnp.swapaxes(up_weight, 1, 2), down_weight)
     sums = [
         jnp.einsum(
             "tes,esd->td",
@@ -540,9 +589,11 @@
         shape(block, bf16),
         [
             pltpu.VMEM((count,) + block, bf16),
-            pltpu.VMEM((count - 1,) + block, bf16),
-            pltpu.VMEM((count - 1,) + block, bf16),
-            dma(count), dma(count), dma(count - 1), dma(count - 1),
+            pltpu.VMEM((reach,) + block, bf16),
+            pltpu.VMEM((reach,) + block, bf16),
+            pltpu.VMEM((reach - 1,) + block, bf16),
+            pltpu.VMEM((reach - 1,) + block, bf16),
+            dma(count), dma(count), dma(reach), dma(reach), dma(reach - 1), dma(reach - 1),
         ],
         2,
         sums,
@@ -559,7 +610,7 @@
     def layer(*args):
         tokens, model = args[2].shape
         fits = count * tokens * model * 2 <= LEAN_BYTES
-        even = count % 2 == 0 and tokens % 32 == 0 and EXPERTS % count == 0
+        even = count % 2 == 0 and count >= 4 and tokens % 32 == 0 and EXPERTS % count == 0
         if fits and even and mesh.shape["tp"] == 2:
             return lean_body(*args)
         return body(*args)

time: 178 us -> 122 us (0.69)
  local copies, waits for them, and re-layouts: 48.8 us -> 9.83 us
  Pallas kernels: 114 us -> 96.9 us
    unnamed x25, local copies, waits for them, and re-layouts: 47.2 us -> 8.24 us
    pallas_call x3, Pallas kernels: 96.7 us -> 79.4 us  [vmem_call(): pl.pallas_call(kernel, out_shape=outs, in_specs=[whole] * len(args), out_...]
where the time goes in v2:
time: 122 us; the launch traced here: 120 us
  Pallas kernels  96.9 us (79%)
  matrix products  12.4 us (10%)
  local copies, waits for them, and re-layouts  9.83 us (8%)
    pallas_call x3, Pallas kernels, vmem_call(): pl.pallas_call(kernel, out_shape=outs, in_specs=[whole] * len(args), out_...  79.4 us
    pallas_call x1, Pallas kernels, lean_body(): pl.pallas_call(functools.partial(expert_kernel, blocks), grid=(local,), o...  17.5 us
    unnamed x25, local copies, waits for them, and re-layouts  8.24 us
    sub x1, matrix products, weighted_rows(): weights = jnp.exp(scores - row_peak[:, :, None]).astype(jnp.bfloat16)  4.82 us
    dot_general x1, matrix products, lean_body(): jnp.einsum('thl,hlv->thv', context, values.reshape(heads, LATENT, VDIM),...  2.87 us

profile of v2, /device:TPU:11, one launch (start us, length us, event | category | flops | bytes accessed | tf_op | source)
XLA Modules:
  0.0 120.5 jit_solution(3834780633240102613)
XLA Ops:
  0.7 1.6 %copy.27.cache_ref = bf16[3,256,576]{2,1,0:T(8,128)(2,1)S(1)} copy(bf16[3,256,576]{1,2,0:T(8,128)(2,1)} %param.14) | data formatting | bytes 1769472 | tf_op args[1]
  2.3 0.8 copy.26
  3.2 0.9 copy-done.2
  4.1 15.4 %shard_map.140 = (bf16[3,2,256,576]{3,2,1,0:T(8,128)(2,1)S(1)}, bf16[8,8,64,128]{3,2,1,0:T(8,128)(2,1)S(1)}, s32[8,8,128]{2,1,0:T(8,128)S(1)}) custom-call(bf16[3,256,576]{2,1,0:T(8,128)(2,1)S(1)} %copy.27.cache_ref, bf16[8,64,128]{2,1,0:T(8,128)(2,1)S(1)} %copy-done.2, s32[8,128]{1,0:T(8,128)S(1)} %pad_bitcast_fusion.ids_ref), custom_call_target="tpu_custom_call" | custom-call | tf_op jit(solution)/shard_map/pallas_call | solution.py:443
  19.5 0.6 copy-done.3
  20.1 1.3 %copy-done.5 = bf16[3,2,256,576]{3,2,1,0:T(8,128)(2,1)} copy-done((bf16[3,2,256,576]{3,2,1,0:T(8,128)(2,1)}, bf16[3,2,256,576]{3,2,1,0:T(8,128)(2,1)S(1)}, u32[]{:S(2)}) %copy-start.5) | copy-done | bytes 1769496
  21.4 1.0 copy-done.7
  22.4 0.1 compare_and_fusion
  22.5 4.8 %convert_reduce_fusion = (f32[64,8]{0,1:T(8,128)S(1)}, bf16[64,8,1536]{2,0,1:T(8,128)(2,1)}) fusion(bf16[1536,576,1]{1,0,2:T(8,128)(2,1)} %bitcast.65, pred[64,1536]{1,0:T(8,128)(4,1)S(1)} %compare_and_fusion, bf16[64,8,576]{2,1,0:T(8,128)(2,1)S(1)} %copy-done), kind=kOutput, calls=%fused_computation.3 | convolution fusion | flops 910689792 | bytes 4032512 | tf_op jit(solution)/shard_map/sub | solution.py:41
  27.4 2.9 %fusion.4 = bf16[8,8,8,128]{3,2,1,0:T(8,128)(2,1)S(1)} fusion(bf16[8,512,128]{2,1,0:T(8,128)(2,1)} %bitcast.67, bf16[64,8,1536]{2,0,1:T(8,128)(2,1)} %get-tuple-element.15, bf16[1536,576]{1,0:T(8,128)(2,1)S(1)} %bitcast.66, f32[64,8]{0,1:T(8,128)S(1)} %get-tuple-element.14), kind=kOutput, calls=%fused_computation.14 | convolution fusion | flops 873005056 | bytes 4329472 | tf_op jit(solution)/shard_map/thl,hlv->thv/dot_general | solution.py:505
  30.3 0.9 constant_dynamic-slice_fusion.1.residual_ref
  31.2 42.1 %shard_map.141 = (bf16[8,2,32,2048]{3,2,1,0:T(8,128)(2,1)S(1)}, bf16[2,32,1024]{2,1,0:T(8,128)(2,1)S(1)}) custom-call(bf16[64,1024]{1,0:T(8,128)(2,1)S(1)} %bitcast.61, bf16[1024,256]{1,0:T(8,128)(2,1)S(1)} %copy-done.1, bf16[32,2048]{1,0:T(8,128)(2,1)S(1)} %constant_dynamic-slice_fusion.1.residual_ref, f32[1,2048]{1,0:T(1,128)S(1)} %bitcast.64), custom_call_target="tpu_custom_call" | custom-call | tf_op jit(solution)/shard_map/pallas_call | solution.py:443
  73.3 0.8 copy.47
  74.1 0.2 eq.52
  74.5 1.7 %fusion.49 = (f32[512]{0:T(512)S(1)}, f32[512,64]{0,1:T(8,128)S(1)}) fusion(pred[512,64]{0,1:T(8,128)(4,1)S(1)} %fusion.14, bf16[512,2048]{1,0:T(8,128)(2,1)S(1)} %bitcast.59, bf16[2048,64]{0,1:T(8,128)(2,1)} %param.21), kind=kOutput, calls=%fused_computation.73 | convolution fusion | flops 134282752 | bytes 2525184 | tf_op jit(solution)/shard_map/dot_general | solution.py:538
  76.4 0.2 fusion.6
  76.7 1.3 %convolution_convert_fusion.rows_ref = bf16[8,64,2048]{2,1,0:T(8,128)(2,1)S(1)} fusion(bf16[512,2048,1]{1,0,2:T(8,128)(2,1)S(1)} %bitcast.60, s32[512,8]{0,1:T(8,128)S(1)} %eq.56, pred[512,8]{0,1:T(8,128)(4,1)S(1)} %constant_dynamic-slice_fusion), kind=kOutput, calls=%fused_computation.5 | convolution fusion | flops 1075314688 | bytes 4214784 | tf_op jit(solution)/shard_map/tes,td->esd/dot_general | solution.py:556
  78.0 17.5 %shard_map.142 = bf16[8,64,2048]{2,1,0:T(8,128)(2,1)S(1)} custom-call(bf16[8,64,2048]{2,1,0:T(8,128)(2,1)S(1)} %convolution_convert_fusion.rows_ref, bf16[16,192,2048]{2,1,0:T(8,128)(2,1)} %bitcast.68, bf16[16,192,2048]{2,1,0:T(8,128)(2,1)} %bitcast.69, bf16[16,192,2048]{2,1,0:T(8,128)(2,1)} %down_ref.1), custom_call_target="tpu_custom_call" | custom-call | tf_op jit(solution)/shard_map/pallas_call | solution.py:563
  95.5 0.8 bitcast_convert_fusion.1
  96.2 0.8 bitcast_convert_fusion
  97.0 0.2 pad_maximum_fusion.sums_ref
  97.2 22.0 %shard_map.143 = bf16[64,1024]{1,0:T(8,128)(2,1)S(1)} custom-call(bf16[2,8,64,1024]{3,2,1,0:T(8,128)(2,1)S(1)} %pad_maximum_fusion.sums_ref), custom_call_target="tpu_custom_call" | custom-call | tf_op jit(solution)/shard_map/pallas_call | solution.py:443
  119.2 0.7 copy.50
  119.8 0.7 copy.51
  (31 shorter events, 0.7 us)
Async XLA Ops:
  0.6 21.9 %copy-start = (bf16[64,8,576]{2,1,0:T(8,128)(2,1)S(1)}, bf16[64,8,576]{2,1,0:T(8,128)(2,1)}, u32[]{:S(2)}) copy-start(bf16[64,8,576]{2,1,0:T(8,128)(2,1)} %param.13) | copy-start | bytes 1769476
  0.6 21.7 %copy-start.9 = (s32[64]{0:T(128)S(1)}, s32[64]{0:T(128)}, u32[]{:S(2)}) copy-start(s32[64]{0:T(128)} %param.16) | copy-start | bytes 772
  0.7 21.7 %copy-start.8 = (s32[64]{0:T(128)S(1)}, s32[64]{0:T(128)}, u32[]{:S(2)}) copy-start(s32[64]{0:T(128)} %param.17) | copy-start | bytes 772
  3.2 0.9 copy-start.2
  19.5 0.6 copy-start.3
  20.1 1.3 %copy-start.5 = (bf16[3,2,256,576]{3,2,1,0:T(8,128)(2,1)}, bf16[3,2,256,576]{3,2,1,0:T(8,128)(2,1)S(1)}, u32[]{:S(2)}) copy-start(bf16[3,2,256,576]{3,2,1,0:T(8,128)(2,1)S(1)} %get-tuple-element.8) | copy-start | bytes 5308420
  21.4 1.0 copy-start.7
  22.5 4.8 %copy-start.6 = (bf16[3,2,256,576]{3,2,1,0:T(8,128)(2,1)S(1)}, bf16[3,2,256,576]{3,2,1,0:T(8,128)(2,1)}, u32[]{:S(2)}) copy-start(bf16[3,2,256,576]{3,2,1,0:T(8,128)(2,1)} %copy-done.5) | copy-start | bytes 5308420
  27.4 3.8 %copy-start.1 = (bf16[1024,256]{1,0:T(8,128)(2,1)S(1)}, bf16[1024,256]{1,0:T(8,128)(2,1)}, u32[]{:S(2)}) copy-start(bf16[1024,256]{1,0:T(8,128)(2,1)} %proj_ref.1) | copy-start | bytes 1572868
  27.4 3.9 %copy-start.4 = (f32[2048]{0:T(1024)S(1)}, f32[2048]{0:T(1024)}, u32[]{:S(2)}) copy-start(f32[2048]{0:T(1024)} %param.20) | copy-start | bytes 24580
